TPU v7x, 256 devices: a whole 4x4x8 slice. The times are simulated.
256 devices in a mesh: win: 32 (over y, x, core), grp: 8 (over z).
Axes of the slice: x: 4, y: 4, z: 8, core: 2. Of those that a mesh axis runs over, the one named last changes fastest.
Arguments:
- traces: bfloat16 [256, 512, 2048], P(('win', 'grp'))
- pair_lists: int32 [32, 3], P('win'), may hold values from -1 to 3, as said below
- observed: float32 [32, 3, 16, 16, 2048], P('win'), may hold values from -4 to 4
Outputs:
- correl: float32 [32, 3, 16, 16, 2048], P('win', None, None, None, 'grp')
- trace_gradient: bfloat16 [256, 512, 2048], P(('win', 'grp'))
Inputs may be any that keep to these rules, and one draw needn't show every extreme that they name: `pair_lists`: each row lists distinct offsets in increasing order, followed by -1 in its empty slots; block a lists only offsets o with a + o < 32; every block lists at least one offset, and block 0 fills all 3 slots and lists offset 4 - 1.
All inputs are finite; a program needn't handle non-finite values.
Results may differ from a plain program's by a relative error of at most 0.014.
Values may be sent and summed in bfloat16 or wider, within the bound.
No kernel may reach another device: no remote copies, remote signals or barrier semaphores. Data moves between devices by JAX's collectives and lax.ppermute only.
A program may use at most 192 MiB of HBM per device.

v0:
```python
import math
import jax
import jax.numpy as jnp
from jax import lax
from jax.sharding import PartitionSpec as P

SEG = 2048
FREQ = 1024
BAND = 64
OFFSETS = 4


def passed_along(array, axis, by):
    peers = lax.axis_size(axis)
    pairs = [(i, i + by) for i in range(peers) if 0 <= i + by < peers]
    return lax.ppermute(array, axis, pairs)


def dft_table(first_column, column_count):
    samples = jnp.arange(SEG, dtype=jnp.int32)
    columns = first_column + jnp.arange(column_count, dtype=jnp.int32)
    harmonic = columns % FREQ
    phases = samples[:, None] * harmonic[None, :] % SEG
    angles = phases.astype(jnp.float32) * (2.0 * math.pi / SEG)
    values = jnp.where(columns[None, :] < FREQ, jnp.cos(angles), -jnp.sin(angles))
    return values.astype(jnp.bfloat16)


def whiten(spectrum):
    halfway = spectrum.shape[-1] // 2
    real_part = spectrum[..., :halfway]
    imag_part = spectrum[..., halfway:]
    power_bins = real_part * real_part + imag_part * imag_part
    banded = power_bins.reshape(power_bins.shape[:-1] + (halfway // BAND, BAND))
    inverse = lax.rsqrt(jnp.mean(banded, axis=-1) + 1e-05)
    spread = jnp.broadcast_to(inverse[..., None], banded.shape).reshape(power_bins.shape)
    return spectrum * jnp.concatenate([spread, spread], axis=-1)


def split_halves(operand):
    halfway = operand.shape[-1] // 2
    return (operand[..., :halfway], operand[..., halfway:])


def widen(operand):
    return operand.astype(jnp.float32)


def correlate(leading, trailing, windows_total):
    lead_real, lead_imag = split_halves(leading)
    trail_real, trail_imag = split_halves(trailing)
    left_real = widen(lead_real)[:, :, None, :]
    left_imag = widen(lead_imag)[:, :, None, :]
    right_real = widen(trail_real)[:, None, :, :]
    right_imag = widen(trail_imag)[:, None, :, :]
    real_sum = jnp.sum(left_real * right_real + left_imag * right_imag, axis=0)
    imag_sum = jnp.sum(left_real * right_imag - left_imag * right_real, axis=0)
    return jnp.concatenate([real_sum, imag_sum], axis=-1) / windows_total


def pull_first(residual, trailing):
    resid_real, resid_imag = split_halves(residual)
    trail_real, trail_imag = split_halves(trailing)
    left_real = widen(resid_real)[None]
    left_imag = widen(resid_imag)[None]
    right_real = widen(trail_real)[:, None, :, :]
    right_imag = widen(trail_imag)[:, None, :, :]
    real_part = jnp.sum(left_real * right_real + left_imag * right_imag, axis=2)
    imag_part = jnp.sum(left_real * right_imag - left_imag * right_real, axis=2)
    return jnp.concatenate([real_part, imag_part], axis=-1)


def pull_second(residual, leading):
    resid_real, resid_imag = split_halves(residual)
    lead_real, lead_imag = split_halves(leading)
    left_real = widen(resid_real)[None]
    left_imag = widen(resid_imag)[None]
    right_real = widen(lead_real)[:, :, None, :]
    right_imag = widen(lead_imag)[:, :, None, :]
    real_part = jnp.sum(left_real * right_real - left_imag * right_imag, axis=1)
    imag_part = jnp.sum(left_real * right_imag + left_imag * right_real, axis=1)
    return jnp.concatenate([real_part, imag_part], axis=-1)


def on_device(traces, pair_lists, observed):
    win_dev, channels, samples = traces.shape
    column_total = 2 * FREQ
    column_step = min(512, column_total)
    tables = [
        dft_table(start_col, column_step) for start_col in range(0, column_total, column_step)
    ]
    flat_traces = traces.reshape(win_dev * channels, samples)
    spectra = jnp.concatenate(
        [
            jnp.dot(flat_traces, table_part, preferred_element_type=jnp.float32)
            for table_part in tables
        ],
        axis=1,
    )
    spectra = spectra.reshape(win_dev, channels, column_total)
    whitened = whiten(spectra).astype(jnp.bfloat16)
    grp_count = lax.axis_size("grp")
    share_width = column_total // grp_count
    moved_blocks = lax.all_to_all(whitened, "win", split_axis=1, concat_axis=0, tiled=True)
    windows_total = moved_blocks.shape[0] * grp_count
    partner_list = [moved_blocks] + [
        passed_along(moved_blocks, "win", -offset) for offset in range(1, OFFSETS)
    ]
    stacked = jnp.stack(partner_list)
    offsets = pair_lists[0]
    slot_total = offsets.shape[0]
    live_slots = (offsets >= 0).astype(jnp.float32)[:, None, None, None]
    partners = [
        lax.dynamic_index_in_dim(stacked, jnp.maximum(offsets[slot_index], 0), 0, keepdims=False)
        for slot_index in range(slot_total)
    ]
    correl = (
        jnp.stack(
            [correlate(moved_blocks, partner_block, windows_total) for partner_block in partners]
        )
        * live_slots
    )
    share_start = lax.axis_index("grp") * share_width
    totals = lax.psum(correl, "grp")
    correl_share = lax.dynamic_slice_in_dim(totals, share_start, share_width, 3)
    residual = ((totals - observed[0]) * live_slots).astype(jnp.bfloat16)
    own_grad = pull_first(residual[0], partners[0])
    for slot_index in range(1, slot_total):
        own_grad = own_grad + pull_first(residual[slot_index], partners[slot_index])
    contrib = []
    for offset in range(OFFSETS):
        chosen = jnp.zeros_like(residual[0])
        for slot_index in range(slot_total):
            chosen = jnp.where(offsets[slot_index] == offset, residual[slot_index], chosen)
        contrib.append(pull_second(chosen, moved_blocks))
    white_grad = own_grad + contrib[0]
    for offset in range(1, OFFSETS):
        white_grad = white_grad + passed_along(
            contrib[offset].astype(jnp.bfloat16), "win", offset
        ).astype(jnp.float32)
    returned = lax.all_to_all(
        white_grad.astype(jnp.bfloat16), "win", split_axis=0, concat_axis=1, tiled=True
    )
    unused, pullback = jax.vjp(whiten, spectra)
    spectra_grad = pullback(returned.astype(jnp.float32))[0].astype(jnp.bfloat16)
    flat_grad = spectra_grad.reshape(win_dev * channels, column_total)
    trace_grad = jnp.zeros((win_dev * channels, samples), jnp.float32)
    for table_index in range(len(tables)):
        start_col = table_index * column_step
        trace_grad = trace_grad + jnp.dot(
            flat_grad[:, start_col : start_col + column_step],
            tables[table_index].T,
            preferred_element_type=jnp.float32,
        )
    return (correl_share[None], trace_grad.reshape(win_dev, channels, samples).astype(jnp.bfloat16))


def solution(mesh):
    return jax.shard_map(
        on_device,
        mesh=mesh,
        in_specs=(P(("win", "grp"), None, None), P("win", None), P("win", None, None, None, None)),
        out_specs=(P("win", None, None, None, "grp"), P(("win", "grp"), None, None)),
        check_vma=False,
    )
```

profile of v0, /device:TPU:1, one launch (start us, length us, event | category | flops | bytes accessed | tf_op | source)
XLA Modules:
  0.0 817.0 jit_solution(5095351248463171921)
XLA Ops:
  7.3 1.4 copy-done
  8.8 17.5 %fusion.41 = f32[512,512]{1,0:T(8,128)S(1)} fusion(bf16[1,512,2048]{2,1,0:T(8,128)(2,1)S(1)} %copy-done, s32[512]{0:T(512)S(1)} %add_select_fusion.4, pred[512]{0:T(512)(128)(4,1)S(1)} %fusion.60), kind=kOutput, calls=%fused_computation.95 | convolution fusion | flops 1091567616 | bytes 3148288 | tf_op jit(solution)/shard_map/dot_general | solution.py:95
  26.2 17.2 %fusion.43 = f32[512,512]{1,0:T(8,128)S(1)} fusion(bf16[1,512,2048]{2,1,0:T(8,128)(2,1)S(1)} %copy-done, s32[512]{0:T(512)S(1)} %add_select_fusion.5, pred[512]{0:T(512)(128)(4,1)S(1)} %fusion.61), kind=kOutput, calls=%fused_computation.97 | convolution fusion | flops 1091567616 | bytes 3148288 | tf_op jit(solution)/shard_map/dot_general | solution.py:95
  43.4 17.6 %fusion.45 = f32[512,512]{1,0:T(8,128)S(1)} fusion(bf16[1,512,2048]{2,1,0:T(8,128)(2,1)S(1)} %copy-done, s32[512]{0:T(512)S(1)} %add_select_fusion.6, pred[512]{0:T(512)(128)(4,1)S(1)} %fusion.62), kind=kOutput, calls=%fused_computation.99 | convolution fusion | flops 1091567616 | bytes 3148288 | tf_op jit(solution)/shard_map/dot_general | solution.py:95
  61.0 17.2 %fusion.47 = f32[512,512]{1,0:T(8,128)S(1)} fusion(bf16[1,512,2048]{2,1,0:T(8,128)(2,1)S(1)} %copy-done, s32[512]{0:T(512)S(1)} %add_select_fusion.7, pred[512]{0:T(512)(128)(4,1)S(1)} %iota_compare_fusion), kind=kOutput, calls=%fused_computation.101 | convolution fusion | flops 1091567616 | bytes 3148288 | tf_op jit(solution)/shard_map/dot_general | solution.py:95
  79.2 2.0 copy-done.3
  82.7 3.9 fusion.16
  86.6 10.8 %copy.14 = bf16[1,512,2048]{2,0,1:T(2,128)(2,1)} copy(bf16[1,512,2048]{1,2,0:T(8,128)(2,1)} %fusion.16) | data formatting | bytes 4194304 | tf_op jit(solution)/shard_map/convert_element_type | solution.py:101
  98.0 13.2 %reduce.2 = bf16[512,2048]{1,0:T(8,128)(2,1)S(1)} reduce(bf16[512,1,2048]{2,1,0:T(2,128)(2,1)} %bitcast.118, bf16[]{:T(256)} %broadcast.306), dimensions={1}, to_apply=%bitcast.108.reduce_sub_computation | reduce | bytes 4194306
  111.1 2.8 reshape.499
  113.9 37.0 %all_to_all.21 = bf16[32,2,16384]{2,1,0:T(2,128)(2,1)S(1)} all-to-all(bf16[32,2,16384]{2,1,0:T(2,128)(2,1)} %reshape.499), channel_id=1, replica_groups=mesh['win'=32,'grp'=8] {'win'}, dimensions={0} | all-to-all | bytes 4194304 | tf_op jit(solution)/shard_map/all_to_all | solution.py:104
  150.9 6.8 reshape.500
  157.6 3.5 copy.17
  163.7 2.3 collective-permute-start
  168.5 2.5 slice_convert_fusion.7
  171.1 18.9 %collective-permute-done.2 = bf16[32,16,2048]{2,1,0:T(8,128)(2,1)S(1)} collective-permute-done((bf16[32,16,2048]{2,1,0:T(8,128)(2,1)S(1)}, bf16[32,16,2048]{2,1,0:T(8,128)(2,1)S(1)}, u32[]{:S(2)}, u32[]{:S(2)}) %collective-permute-start.2) | collective-permute-done | bytes 2097184 | tf_op jit(solution)/shard_map/ppermute | solution.py:16
  190.0 63.7 %collective-permute-done.1 = bf16[32,16,2048]{2,1,0:T(8,128)(2,1)S(1)} collective-permute-done((bf16[32,16,2048]{2,1,0:T(8,128)(2,1)S(1)}, bf16[32,16,2048]{2,1,0:T(8,128)(2,1)S(1)}, u32[]{:S(2)}, u32[]{:S(2)}) %collective-permute-start.1) | collective-permute-done | bytes 2097184 | tf_op jit(solution)/shard_map/ppermute | solution.py:16
  253.7 1.9 collective-permute-done
  257.8 1.8 slice_convert_fusion.6
  259.6 3.7 slice_convert_fusion
  263.3 35.8 %add_reduce_fusion.9 = (f32[16,16,1024]{2,1,0:T(8,128)}, f32[16,16,1024]{2,1,0:T(8,128)}, f32[16,16,1024]{2,1,0:T(8,128)}, f32[16,16,1024]{2,1,0:T(8,128)}, f32[16,16,1024]{2,1,0:T(8,128)}, /*index=5*/f32[16,16,1024]{2,1,0:T(8,128)}) fusion(f32[32,16,1024]{2,1,0:T(8,128)} %get-tuple-element.50, f32[32,16,1024]{2,1,0:T(8,128)} %get-tuple-element.48, ...), kind=kLoop, calls=%fused_computation.19 | loop fusion | flops 199753728 | bytes 23068672 | tf_op jit(solution)/shard_map/reduce_sum | solution.py:56
  299.1 1.8 maximum_multiply_fusion.1
  302.1 3.4 maximum_multiply_fusion
  313.0 164.2 %all-reduce.4.cloned.1.call-done = f32[3,16,16,2048]{3,2,1,0:T(8,128)} async-done(((f32[3,16,16,2048]{3,2,1,0:T(8,128)}), f32[3,16,16,2048]{3,2,1,0:T(8,128)}) %all-reduce.4.cloned.1.call-update) | async-done | bytes 6291472 | tf_op jit(solution)/shard_map/psum | solution.py:124
  477.2 6.4 fusion.1
  488.2 70.5 %subtract_reduce_fusion.2 = (bf16[32,16,1024]{2,1,0:T(8,128)(2,1)S(1)}, bf16[32,16,1024]{2,1,0:T(8,128)(2,1)S(1)}, f32[32,16,1024]{2,1,0:T(8,128)S(1)}, f32[32,1...) fusion(f32[16,16,1024]{2,1,0:T(8,128)S(1)} %get-tuple-element.5, ...), kind=kLoop, calls=%fused_computation.5 | loop fusion | flops 264241152 | bytes 23068672 | tf_op jit(solution)/shard_map/reduce_sum | solution.py:80
  558.7 1.9 pad_maximum_fusion.5
  560.6 6.5 collective-permute-start.5
  567.3 3.0 collective-permute-start.4
  570.3 1.5 pad_maximum_fusion.3
  571.7 1.9 collective-permute-start.3
  573.7 20.6 %add_reduce_fusion.4 = (f32[32,16,1024]{2,1,0:T(8,128)S(1)}, f32[32,16,1024]{2,1,0:T(8,128)S(1)}) fusion(f32[16,16,1024]{2,1,0:T(8,128)S(1)} %get-tuple-element.60, f32[16,16,1024]{2,1,0:T(8,128)S(1)} %get-tuple-element.59, f32[32,16,1024]{2,1,0:T(8,128)S(1)} %copy-done.9, f32[32,16,1024]{2,1,0:T(8,128)S(1)} %copy-done.10), kind=kLoop, calls=%fused_computation.9 | loop fusion | flops 66060288 | bytes 10485760 | tf_op jit(solution)/shard_map/reduce_sum | solution.py:68
  594.3 20.6 %add_reduce_fusion.5 = (f32[32,16,1024]{2,1,0:T(8,128)S(1)}, f32[32,16,1024]{2,1,0:T(8,128)S(1)}) fusion(f32[16,16,1024]{2,1,0:T(8,128)S(1)} %get-tuple-element.62, f32[16,16,1024]{2,1,0:T(8,128)S(1)} %get-tuple-element.61, f32[32,16,1024]{2,1,0:T(8,128)S(1)} %copy-done.8, f32[32,16,1024]{2,1,0:T(8,128)S(1)} %copy-done.7), kind=kLoop, calls=%fused_computation.11 | loop fusion | flops 66060288 | bytes 10485760 | tf_op jit(solution)/shard_map/reduce_sum | solution.py:68
  616.5 20.5 %add_reduce_fusion.6 = (f32[32,16,1024]{2,1,0:T(8,128)S(1)}, f32[32,16,1024]{2,1,0:T(8,128)S(1)}) fusion(f32[16,16,1024]{2,1,0:T(8,128)S(1)} %get-tuple-element.64, f32[16,16,1024]{2,1,0:T(8,128)S(1)} %get-tuple-element.63, f32[32,16,1024]{2,1,0:T(8,128)S(1)} %copy-done.4, f32[32,16,1024]{2,1,0:T(8,128)S(1)} %get-tuple-element.49), kind=kLoop, calls=%fused_computation.13 | loop fusion | flops 66060288 | bytes 10485760 | tf_op jit(solution)/shard_map/reduce_sum | solution.py:68
  637.1 17.6 %collective-permute-done.4 = bf16[32,16,2048]{2,1,0:T(8,128)(2,1)} collective-permute-done((bf16[32,16,2048]{2,1,0:T(8,128)(2,1)S(1)}, bf16[32,16,2048]{2,1,0:T(8,128)(2,1)}, u32[]{:S(2)}, u32[]{:S(2)}) %collective-permute-start.4) | collective-permute-done | bytes 2097184 | tf_op jit(solution)/shard_map/ppermute | solution.py:16
  654.6 22.6 %collective-permute-done.3 = bf16[32,16,2048]{2,1,0:T(8,128)(2,1)} collective-permute-done((bf16[32,16,2048]{2,1,0:T(8,128)(2,1)}, bf16[32,16,2048]{2,1,0:T(8,128)(2,1)}, u32[]{:S(2)}, u32[]{:S(2)}) %collective-permute-start.3) | collective-permute-done | bytes 2097184 | tf_op jit(solution)/shard_map/ppermute | solution.py:16
  677.2 5.7 fusion.25
  682.9 8.8 %all-to-all-start.1 = ((bf16[32,16,2048]{2,1,0:T(8,128)(2,1)}), bf16[32,16,2048]{2,1,0:T(8,128)(2,1)S(1)}, u32[]{:S(2)}, u32[]{:S(2)}) async-start(bf16[32,16,2048]{2,1,0:T(8,128)(2,1)} %fusion.25), calls=%async_computation.1 | async-start | bytes 4194304 | tf_op jit(solution)/shard_map/all_to_all | solution.py:141
  691.7 2.1 dynamic-slice_bitcast_fusion.3
  693.8 25.7 %all-to-all-done.1 = bf16[32,16,2048]{2,1,0:T(8,128)(2,1)S(1)} async-done(((bf16[32,16,2048]{2,1,0:T(8,128)(2,1)}), bf16[32,16,2048]{2,1,0:T(8,128)(2,1)S(1)}, u32[]{:S(2)}, u32[]{:S(2)}) %all-to-all-start.1) | async-done | bytes 2097184 | tf_op jit(solution)/shard_map/all_to_all | solution.py:141
  719.4 2.5 bitcast_convert_fusion
  721.9 5.5 copy.15
  727.4 3.5 fusion.39
  731.8 2.9 bitcast_multiply_fusion.1
  737.3 17.7 %fusion.49 = f32[512,2048]{1,0:T(8,128)S(1)} fusion(s32[512]{0:T(512)S(1)} %add_select_fusion.5, pred[512]{0:T(512)(128)(4,1)S(1)} %fusion.61, bf16[512,2048]{0,1:T(8,128)(2,1)S(1)} %fusion.40), kind=kOutput, calls=%fused_computation.107 | convolution fusion | flops 1091567616 | bytes 4721152 | tf_op jit(solution)/shard_map/dot_general | solution.py:150
  755.0 17.8 %fusion.50 = f32[512,2048]{1,0:T(8,128)S(1)} fusion(s32[512]{0:T(512)S(1)} %add_select_fusion.6, pred[512]{0:T(512)(128)(4,1)S(1)} %fusion.62, bf16[512,2048]{0,1:T(8,128)(2,1)S(1)} %fusion.40), kind=kOutput, calls=%fused_computation.108 | convolution fusion | flops 1091567616 | bytes 4721152 | tf_op jit(solution)/shard_map/dot_general | solution.py:150
  772.8 18.1 %fusion.51 = f32[512,2048]{1,0:T(8,128)S(1)} fusion(s32[512]{0:T(512)S(1)} %add_select_fusion.7, pred[512]{0:T(512)(128)(4,1)S(1)} %iota_compare_fusion, bf16[512,2048]{0,1:T(8,128)(2,1)S(1)} %fusion.40), kind=kOutput, calls=%fused_computation.109 | convolution fusion | flops 1091567616 | bytes 4721152 | tf_op jit(solution)/shard_map/dot_general | solution.py:150
  791.0 19.0 %fusion.38 = bf16[1,512,2048]{2,1,0:T(8,128)(2,1)} fusion(f32[512,2048]{1,0:T(8,128)S(1)} %fusion.49, f32[512,2048]{1,0:T(8,128)S(1)} %fusion.51, f32[512,2048]{1,0:T(8,128)S(1)} %fusion.50, s32[512]{0:T(512)S(1)} %add_select_fusion.4, pred[512]{0:T(512)(128)(4,1)S(1)} %fusion.60, bf16[512,2048]{0,1:T(8,128)(2,1)S(1)} %fusion.40), kind=kOutput, calls=%fused_computation.84 | convolution fusion | flops 1095761920 | bytes 15206912 | tf_op jit(solution)/shard_map/dot_general | solution.py:150
  (90 shorter events, 19.3 us)
Async XLA Ops:
  7.2 1.6 copy-start
  7.2 470.0 %all-reduce.4.cloned.1.call-start = ((), (), s32[]{:S(2)}) async-start(), calls=%async_computation.2 | async-start | bytes 12582912 | tf_op jit(solution)/shard_map/psum | solution.py:124
  43.4 34.8 %copy-start.13 = (f32[512,512]{1,0:T(8,128)}, f32[512,512]{1,0:T(8,128)S(1)}, u32[]{:S(2)}) copy-start(f32[512,512]{1,0:T(8,128)S(1)} %fusion.43) | copy-start | bytes 3145732
  61.0 17.2 %copy-start.15 = (f32[512,512]{1,0:T(8,128)}, f32[512,512]{1,0:T(8,128)S(1)}, u32[]{:S(2)}) copy-start(f32[512,512]{1,0:T(8,128)S(1)} %fusion.45) | copy-start | bytes 3145732
  78.2 1.0 copy-start.17
  79.2 2.0 copy-start.3
  82.6 3.9 copy-start.5
  157.6 8.4 %copy-start.25 = (s32[1,3]{1,0:T(1,128)S(1)}, s32[1,3]{1,0:T(1,128)}, u32[]{:S(2)}) copy-start(s32[1,3]{1,0:T(1,128)} %param.4) | copy-start | bytes 40
  161.1 28.9 %collective-permute-start.2 = (bf16[32,16,2048]{2,1,0:T(8,128)(2,1)S(1)}, bf16[32,16,2048]{2,1,0:T(8,128)(2,1)S(1)}, u32[]{:S(2)}, u32[]{:S(2)}) collective-permute-start(bf16[32,16,2048]{2,1,0:T(8,128)(2,1)S(1)} %bitcast.111), channel_id=1, source_target_pairs={{24,0},{32,8},{40,16},{48,24},{56,32},{64,40},{72,48},{80,56},{88,... | collective-permute-start | bytes 6291464 | tf_op jit(solution)/shard_map/ppermute | solution.py:16
  162.4 91.2 %collective-permute-start.1 = (bf16[32,16,2048]{2,1,0:T(8,128)(2,1)S(1)}, bf16[32,16,2048]{2,1,0:T(8,128)(2,1)S(1)}, u32[]{:S(2)}, u32[]{:S(2)}) collective-permute-start(bf16[32,16,2048]{2,1,0:T(8,128)(2,1)S(1)} %bitcast.112), channel_id=1, source_target_pairs={{16,0},{24,8},{32,16},{40,24},{48,32},{56,40},{64,48},{72,56},{80,... | collective-permute-start | bytes 6291464 | tf_op jit(solution)/shard_map/ppermute | solution.py:16
  163.7 91.9 %collective-permute-start = (bf16[32,16,2048]{2,1,0:T(8,128)(2,1)S(1)}, bf16[32,16,2048]{2,1,0:T(8,128)(2,1)S(1)}, u32[]{:S(2)}, u32[]{:S(2)}) collective-permute-start(bf16[32,16,2048]{2,1,0:T(8,128)(2,1)S(1)} %bitcast.113), channel_id=1, source_target_pairs={{8,0},{16,8},{24,16},{32,24},{40,32},{48,40},{56,48},{64,56},{72,6... | collective-permute-start | bytes 6291464 | tf_op jit(solution)/shard_map/ppermute | solution.py:16
  299.1 1.9 copy-start.23
  299.1 2.2 copy-start.24
  299.1 2.5 copy-start.21
  299.1 2.8 copy-start.22
  486.0 1.6 copy-start.11
  486.0 2.2 copy-start.12
  558.7 8.4 %copy-start.19 = (bf16[32,16,1024]{2,1,0:T(8,128)(2,1)S(1)}, bf16[32,16,1024]{2,1,0:T(8,128)(2,1)}, u32[]{:S(2)}) copy-start(bf16[32,16,1024]{2,1,0:T(8,128)(2,1)} %get-tuple-element.24) | copy-start | bytes 3145732
  558.7 8.4 %copy-start.20 = (bf16[32,16,1024]{2,1,0:T(8,128)(2,1)S(1)}, bf16[32,16,1024]{2,1,0:T(8,128)(2,1)}, u32[]{:S(2)}) copy-start(bf16[32,16,1024]{2,1,0:T(8,128)(2,1)} %get-tuple-element.25) | copy-start | bytes 3145732
  560.6 76.5 %collective-permute-start.5 = (bf16[32,16,2048]{2,1,0:T(8,128)(2,1)S(1)}, bf16[32,16,2048]{2,1,0:T(8,128)(2,1)}, u32[]{:S(2)}, u32[]{:S(2)}) collective-permute-start(bf16[32,16,2048]{2,1,0:T(8,128)(2,1)S(1)} %pad_maximum_fusion.5), channel_id=1, source_target_pairs={{0,24},{8,32},{16,40},{24,48},{32,56},{40,64},{48,72},{56,80},{64,... | collective-permute-start | bytes 6291464 | tf_op jit(solution)/shard_map/ppermute | solution.py:16
  567.1 6.6 copy-start.9
  567.1 6.6 copy-start.10
  567.3 87.3 %collective-permute-start.4 = (bf16[32,16,2048]{2,1,0:T(8,128)(2,1)S(1)}, bf16[32,16,2048]{2,1,0:T(8,128)(2,1)}, u32[]{:S(2)}, u32[]{:S(2)}) collective-permute-start(bf16[32,16,2048]{2,1,0:T(8,128)(2,1)S(1)} %pad_maximum_fusion.4), channel_id=1, source_target_pairs={{0,16},{8,24},{16,32},{24,40},{32,48},{40,56},{48,64},{56,72},{64,... | collective-permute-start | bytes 6291464 | tf_op jit(solution)/shard_map/ppermute | solution.py:16
  571.7 105.5 %collective-permute-start.3 = (bf16[32,16,2048]{2,1,0:T(8,128)(2,1)}, bf16[32,16,2048]{2,1,0:T(8,128)(2,1)}, u32[]{:S(2)}, u32[]{:S(2)}) collective-permute-start(bf16[32,16,2048]{2,1,0:T(8,128)(2,1)} %pad_maximum_fusion.3), channel_id=1, source_target_pairs={{0,8},{8,16},{16,24},{24,32},{32,40},{40,48},{48,56},{56,64},{64,7... | collective-permute-start | bytes 6291464 | tf_op jit(solution)/shard_map/ppermute | solution.py:16
  573.7 20.6 %copy-start.7 = (f32[32,16,1024]{2,1,0:T(8,128)S(1)}, f32[32,16,1024]{2,1,0:T(8,128)}, u32[]{:S(2)}) copy-start(f32[32,16,1024]{2,1,0:T(8,128)} %get-tuple-element.68) | copy-start | bytes 6291460
  573.7 20.6 %copy-start.8 = (f32[32,16,1024]{2,1,0:T(8,128)S(1)}, f32[32,16,1024]{2,1,0:T(8,128)}, u32[]{:S(2)}) copy-start(f32[32,16,1024]{2,1,0:T(8,128)} %get-tuple-element.69) | copy-start | bytes 6291460
  594.3 20.6 %copy-start.18 = (bf16[16,16,2048]{2,1,0:T(8,128)(2,1)S(1)}, bf16[16,16,2048]{2,1,0:T(8,128)(2,1)}, u32[]{:S(2)}) copy-start(bf16[16,16,2048]{2,1,0:T(8,128)(2,1)} %get-tuple-element.42) | copy-start | bytes 3145732
  614.9 1.6 copy-start.4
  682.9 36.5 %all-to-all-start.1 = ((bf16[32,16,2048]{2,1,0:T(8,128)(2,1)}), bf16[32,16,2048]{2,1,0:T(8,128)(2,1)S(1)}, u32[]{:S(2)}, u32[]{:S(2)}) async-start(bf16[32,16,2048]{2,1,0:T(8,128)(2,1)} %fusion.25), calls=%async_computation.1 | async-start | bytes 4194304 | tf_op jit(solution)/shard_map/all_to_all | solution.py:141
  721.9 5.5 copy-start.14
  721.9 5.5 copy-start.16
  731.7 3.5 copy-start.2
  731.8 4.1 copy-start.6
  790.9 19.0 %copy-start.1 = (bf16[1,512,2048]{2,1,0:T(8,128)(2,1)S(1)}, bf16[1,512,2048]{2,1,0:T(8,128)(2,1)}, u32[]{:S(2)}) copy-start(bf16[1,512,2048]{2,1,0:T(8,128)(2,1)} %param.3) | copy-start | bytes 6291460
Sparse Core Ops, SparseCore 0:
  305.7 171.4 all-reduce.3
where the time goes:
time: 826 us; the launch traced here: 817 us
  waiting for transfers between devices  315 us (38%)
  other arithmetic  230 us (28%)
  matrix products  142 us (17%)
  local copies, waits for them, and re-layouts  43.9 us (5%)
  blocking collectives  37 us (4%)
  starting transfers between devices  25.1 us (3%)
  between operations  24.1 us (3%)
    psum x1, waiting for transfers between devices, on_device(): totals = lax.psum(correl, 'grp')  164 us
    ppermute x6, waiting for transfers between devices, passed_along(): return lax.ppermute(array, axis, pairs)  125 us
    dot_general x4, matrix products, on_device(): jnp.dot(flat_grad[:, start_col:start_col + column_step], tables[table_ind...  72.6 us
    reduce_sum x1, other arithmetic, pull_second(): real_part = jnp.sum(left_real * right_real - left_imag * right_imag, axis=1)  70.5 us
    dot_general x4, matrix products, on_device(): jnp.dot(flat_traces, table_part, preferred_element_type=jnp.float32)  69.4 us
    reduce_sum x3, other arithmetic, pull_first(): real_part = jnp.sum(left_real * right_real + left_imag * right_imag, axis=2)  61.7 us
    all_to_all x1, blocking collectives, on_device(): lax.all_to_all(whitened, 'win', split_axis=1, concat_axis=0, tiled=True)  37 us
    reduce_sum x1, other arithmetic, correlate(): real_sum = jnp.sum(left_real * right_real + left_imag * right_imag, axis=0)  35.8 us
  transfers between devices with their start and end apart: 8, of which 7 were waited for; matrix products, arithmetic and copies ran while one was open for 8% of the time, Pallas kernels for 0%

commit v1 on v0

--- a/solution.py
+++ b/solution.py
@@ -121,7 +121,7 @@
         * live_slots
     )
     share_start = lax.axis_index("grp") * share_width
-    totals = lax.psum(correl, "grp")
+    totals = jnp.sum(lax.all_gather(correl, "grp"), axis=0)
     correl_share = lax.dynamic_slice_in_dim(totals, share_start, share_width, 3)
     residual = ((totals - observed[0]) * live_slots).astype(jnp.bfloat16)
     own_grad = pull_first(residual[0], partners[0])

time: 826 us -> 1190 us (1.44)
  waiting for transfers between devices: 315 us -> 654 us
  other arithmetic: 230 us -> 248 us
    all_gather x0 -> x1, waiting for transfers between devices: none -> 546 us  [on_device(): totals = jnp.sum(lax.all_gather(correl, 'grp'), axis=0)]
    psum x1 -> x0, waiting for transfers between devices: 164 us -> none  [on_device(): totals = lax.psum(correl, 'grp')]
    ppermute x6, waiting for transfers between devices: 125 us -> 82.2 us  [passed_along(): return lax.ppermute(array, axis, pairs)]
    reduce_sum x0 -> x1, other arithmetic: none -> 20.4 us  [on_device(): totals = jnp.sum(lax.all_gather(correl, 'grp'), axis=0)]
  transfers between devices with their start and end apart: 8 -> 8, of which waited for: 7 -> 6; matrix products, arithmetic and copies ran while one was open for 8% -> 6% of each run, Pallas kernels for 0% -> 0%
where the time goes in v1:
time: 1190 us; the launch traced here: 1180 us
  waiting for transfers between devices  654 us (55%)
  other arithmetic  248 us (21%)
  matrix products  142 us (12%)
  local copies, waits for them, and re-layouts  44.7 us (4%)
  blocking collectives  37 us (3%)
  starting transfers between devices  25.7 us (2%)
  between operations  24.7 us (2%)
    all_gather x1, waiting for transfers between devices, on_device(): totals = jnp.sum(lax.all_gather(correl, 'grp'), axis=0)  546 us
    ppermute x6, waiting for transfers between devices, passed_along(): return lax.ppermute(array, axis, pairs)  82.2 us
    dot_general x4, matrix products, on_device(): jnp.dot(flat_grad[:, start_col:start_col + column_step], tables[table_ind...  72.6 us
    reduce_sum x1, other arithmetic, pull_second(): real_part = jnp.sum(left_real * right_real - left_imag * right_imag, axis=1)  69.6 us
    dot_general x4, matrix products, on_device(): jnp.dot(flat_traces, table_part, preferred_element_type=jnp.float32)  69.4 us
    reduce_sum x3, other arithmetic, pull_first(): real_part = jnp.sum(left_real * right_real + left_imag * right_imag, axis=2)  61.7 us
    all_to_all x1, blocking collectives, on_device(): lax.all_to_all(whitened, 'win', split_axis=1, concat_axis=0, tiled=True)  37 us
    reduce_sum x1, other arithmetic, correlate(): real_sum = jnp.sum(left_real * right_real + left_imag * right_imag, axis=0)  35.8 us
  transfers between devices with their start and end apart: 8, of which 6 were waited for; matrix products, arithmetic and copies ran while one was open for 6% of the time, Pallas kernels for 0%

profile of v1, /device:TPU:1, one launch (start us, length us, event | category | flops | bytes accessed | tf_op | source)
XLA Modules:
  0.0 1176.3 jit_solution(3680514620451780739)
XLA Ops:
  7.3 1.4 copy-done
  8.8 17.5 %fusion.50 = f32[512,512]{1,0:T(8,128)S(1)} fusion(bf16[1,512,2048]{2,1,0:T(8,128)(2,1)S(1)} %copy-done, s32[512]{0:T(512)S(1)} %add_select_fusion.7, pred[512]{0:T(512)(128)(4,1)S(1)} %iota_compare_fusion), kind=kOutput, calls=%fused_computation.104 | convolution fusion | flops 1091567616 | bytes 3148288 | tf_op jit(solution)/shard_map/dot_general | solution.py:95
  26.2 17.2 %fusion.48 = f32[512,512]{1,0:T(8,128)S(1)} fusion(bf16[1,512,2048]{2,1,0:T(8,128)(2,1)S(1)} %copy-done, s32[512]{0:T(512)S(1)} %add_select_fusion.6, pred[512]{0:T(512)(128)(4,1)S(1)} %fusion.65), kind=kOutput, calls=%fused_computation.102 | convolution fusion | flops 1091567616 | bytes 3148288 | tf_op jit(solution)/shard_map/dot_general | solution.py:95
  43.4 17.6 %fusion.46 = f32[512,512]{1,0:T(8,128)S(1)} fusion(bf16[1,512,2048]{2,1,0:T(8,128)(2,1)S(1)} %copy-done, s32[512]{0:T(512)S(1)} %add_select_fusion.5, pred[512]{0:T(512)(128)(4,1)S(1)} %fusion.64), kind=kOutput, calls=%fused_computation.100 | convolution fusion | flops 1091567616 | bytes 3148288 | tf_op jit(solution)/shard_map/dot_general | solution.py:95
  61.0 17.2 %fusion.44 = f32[512,512]{1,0:T(8,128)S(1)} fusion(bf16[1,512,2048]{2,1,0:T(8,128)(2,1)S(1)} %copy-done, s32[512]{0:T(512)S(1)} %add_select_fusion.4, pred[512]{0:T(512)(128)(4,1)S(1)} %fusion.63), kind=kOutput, calls=%fused_computation.98 | convolution fusion | flops 1091567616 | bytes 3148288 | tf_op jit(solution)/shard_map/dot_general | solution.py:95
  79.3 2.0 copy-done.3
  82.8 4.0 fusion.16
  86.7 10.8 copy.14
  98.1 13.2 %reduce.2 = bf16[512,2048]{1,0:T(8,128)(2,1)S(1)} reduce(bf16[512,1,2048]{2,1,0:T(2,128)(2,1)} %bitcast.124, bf16[]{:T(256)} %broadcast.331), dimensions={1}, to_apply=%bitcast.114.reduce_sub_computation | reduce | bytes 4194306
  111.2 2.8 reshape.595
  114.0 37.0 %all_to_all.21 = bf16[32,2,16384]{2,1,0:T(2,128)(2,1)S(1)} all-to-all(bf16[32,2,16384]{2,1,0:T(2,128)(2,1)} %reshape.595), channel_id=1, replica_groups=mesh['win'=32,'grp'=8] {'win'}, dimensions={0} | all-to-all | bytes 4194304 | tf_op jit(solution)/shard_map/all_to_all | solution.py:104
  151.0 6.8 reshape.596
  157.8 3.5 copy.17
  161.2 2.3 collective-permute-start
  168.8 2.4 slice_convert_fusion.7
  171.2 38.1 %collective-permute-done = bf16[32,16,2048]{2,1,0:T(8,128)(2,1)S(1)} collective-permute-done((bf16[32,16,2048]{2,1,0:T(8,128)(2,1)S(1)}, bf16[32,16,2048]{2,1,0:T(8,128)(2,1)S(1)}, u32[]{:S(2)}, u32[]{:S(2)}) %collective-permute-start) | collective-permute-done | bytes 2097184 | tf_op jit(solution)/shard_map/ppermute | solution.py:16
  209.3 3.9 collective-permute-done.1
  215.4 1.8 slice_convert_fusion.6
  217.2 3.7 slice_convert_fusion
  220.9 35.8 %add_reduce_fusion.9 = (f32[16,16,1024]{2,1,0:T(8,128)}, f32[16,16,1024]{2,1,0:T(8,128)}, f32[16,16,1024]{2,1,0:T(8,128)}, f32[16,16,1024]{2,1,0:T(8,128)}, f32[16,16,1024]{2,1,0:T(8,128)}, /*index=5*/f32[16,16,1024]{2,1,0:T(8,128)}) fusion(f32[32,16,1024]{2,1,0:T(8,128)} %get-tuple-element.50, f32[32,16,1024]{2,1,0:T(8,128)} %get-tuple-element.48, ...), kind=kLoop, calls=%fused_computation.19 | loop fusion | flops 199753728 | bytes 23068672 | tf_op jit(solution)/shard_map/reduce_sum | solution.py:56
  256.7 1.8 fusion.41
  259.7 3.3 maximum_multiply_fusion
  270.9 546.0 %all-gather.2.cloned.1.call-done = f32[8,3,16,16,2048]{4,3,2,1,0:T(8,128)} async-done(((f32[1,3,16,16,2048]{4,3,2,1,0:T(8,128)}), f32[8,3,16,16,2048]{4,3,2,1,0:T(8,128)}) %all-gather.2.cloned.1.call-update) | async-done | bytes 50331664 | tf_op jit(solution)/shard_map/all_gather | solution.py:124
  816.9 20.4 %reduce_sum.222 = f32[3,16,16,2048]{3,2,1,0:T(8,128)} reduce(f32[8,3,16,16,2048]{4,3,2,1,0:T(8,128)} %all-gather.2.cloned.1.call-done, f32[]{:T(128)} %constant.114.clone.1), dimensions={0}, to_apply=%region_7.8 | reduce | flops 11010048 | bytes 56623108 | tf_op jit(solution)/shard_map/reduce_sum | solution.py:124
  837.3 6.4 fusion.1
  843.7 1.6 slice_bitcast_fusion
  848.5 69.6 %subtract_reduce_fusion.2 = (bf16[32,16,1024]{2,1,0:T(8,128)(2,1)}, bf16[32,16,1024]{2,1,0:T(8,128)(2,1)}, f32[32,16,1024]{2,1,0:T(8,128)S(1)}, f32[32,16,1024]{...) fusion(f32[16,16,1024]{2,1,0:T(8,128)S(1)} %get-tuple-element.5, ...), kind=kLoop, calls=%fused_computation.5 | loop fusion | flops 264241152 | bytes 23068672 | tf_op jit(solution)/shard_map/reduce_sum | solution.py:80
  918.1 1.7 pad_maximum_fusion.3
  919.9 3.7 collective-permute-start.3
  923.7 4.5 collective-permute-start.4
  928.5 3.7 collective-permute-start.5
  932.7 20.6 %add_reduce_fusion.4 = (f32[32,16,1024]{2,1,0:T(8,128)S(1)}, f32[32,16,1024]{2,1,0:T(8,128)S(1)}) fusion(f32[16,16,1024]{2,1,0:T(8,128)S(1)} %get-tuple-element.60, f32[16,16,1024]{2,1,0:T(8,128)S(1)} %get-tuple-element.59, f32[32,16,1024]{2,1,0:T(8,128)S(1)} %copy-done.9, f32[32,16,1024]{2,1,0:T(8,128)S(1)} %copy-done.10), kind=kLoop, calls=%fused_computation.9 | loop fusion | flops 66060288 | bytes 10485760 | tf_op jit(solution)/shard_map/reduce_sum | solution.py:68
  953.4 20.6 %add_reduce_fusion.5 = (f32[32,16,1024]{2,1,0:T(8,128)S(1)}, f32[32,16,1024]{2,1,0:T(8,128)S(1)}) fusion(f32[16,16,1024]{2,1,0:T(8,128)S(1)} %get-tuple-element.62, f32[16,16,1024]{2,1,0:T(8,128)S(1)} %get-tuple-element.61, f32[32,16,1024]{2,1,0:T(8,128)S(1)} %copy-done.8, f32[32,16,1024]{2,1,0:T(8,128)S(1)} %copy-done.7), kind=kLoop, calls=%fused_computation.11 | loop fusion | flops 66060288 | bytes 10485760 | tf_op jit(solution)/shard_map/reduce_sum | solution.py:68
  975.6 20.5 %add_reduce_fusion.6 = (f32[32,16,1024]{2,1,0:T(8,128)S(1)}, f32[32,16,1024]{2,1,0:T(8,128)S(1)}) fusion(f32[16,16,1024]{2,1,0:T(8,128)S(1)} %get-tuple-element.64, f32[16,16,1024]{2,1,0:T(8,128)S(1)} %get-tuple-element.63, f32[32,16,1024]{2,1,0:T(8,128)S(1)} %copy-done.4, f32[32,16,1024]{2,1,0:T(8,128)S(1)} %get-tuple-element.49), kind=kLoop, calls=%fused_computation.13 | loop fusion | flops 66060288 | bytes 10485760 | tf_op jit(solution)/shard_map/reduce_sum | solution.py:68
  996.1 14.9 %collective-permute-done.4 = bf16[32,16,2048]{2,1,0:T(8,128)(2,1)} collective-permute-done((bf16[32,16,2048]{2,1,0:T(8,128)(2,1)S(1)}, bf16[32,16,2048]{2,1,0:T(8,128)(2,1)}, u32[]{:S(2)}, u32[]{:S(2)}) %collective-permute-start.4) | collective-permute-done | bytes 2097184 | tf_op jit(solution)/shard_map/ppermute | solution.py:16
  1011.0 25.4 %collective-permute-done.5 = bf16[32,16,2048]{2,1,0:T(8,128)(2,1)} collective-permute-done((bf16[32,16,2048]{2,1,0:T(8,128)(2,1)S(1)}, bf16[32,16,2048]{2,1,0:T(8,128)(2,1)}, u32[]{:S(2)}, u32[]{:S(2)}) %collective-permute-start.5) | collective-permute-done | bytes 2097184 | tf_op jit(solution)/shard_map/ppermute | solution.py:16
  1036.4 5.7 fusion.25
  1042.1 8.9 all-to-all-start.1
  1051.0 2.1 dynamic-slice_bitcast_fusion.3
  1053.0 25.7 %all-to-all-done.1 = bf16[32,16,2048]{2,1,0:T(8,128)(2,1)S(1)} async-done(((bf16[32,16,2048]{2,1,0:T(8,128)(2,1)}), bf16[32,16,2048]{2,1,0:T(8,128)(2,1)S(1)}, u32[]{:S(2)}, u32[]{:S(2)}) %all-to-all-start.1) | async-done | bytes 2097184 | tf_op jit(solution)/shard_map/all_to_all | solution.py:141
  1078.7 2.5 bitcast_convert_fusion
  1081.2 5.5 copy.15
  1086.7 3.5 fusion.39
  1091.0 2.9 bitcast_multiply_fusion.1
  1096.6 17.7 %fusion.53 = f32[512,2048]{1,0:T(8,128)S(1)} fusion(s32[512]{0:T(512)S(1)} %add_select_fusion.6, pred[512]{0:T(512)(128)(4,1)S(1)} %fusion.65, bf16[512,2048]{0,1:T(8,128)(2,1)S(1)} %fusion.40), kind=kOutput, calls=%fused_computation.111 | convolution fusion | flops 1091567616 | bytes 4721152 | tf_op jit(solution)/shard_map/dot_general | solution.py:150
  1114.3 17.8 %fusion.54 = f32[512,2048]{1,0:T(8,128)S(1)} fusion(s32[512]{0:T(512)S(1)} %copy-done.26, pred[512]{0:T(512)(128)(4,1)S(1)} %copy-done.28, bf16[512,2048]{0,1:T(8,128)(2,1)S(1)} %fusion.40), kind=kOutput, calls=%fused_computation.112 | convolution fusion | flops 1091567616 | bytes 4721152 | tf_op jit(solution)/shard_map/dot_general | solution.py:150
  1132.1 18.1 %fusion.52 = f32[512,2048]{1,0:T(8,128)S(1)} fusion(s32[512]{0:T(512)S(1)} %add_select_fusion.5, pred[512]{0:T(512)(128)(4,1)S(1)} %fusion.64, bf16[512,2048]{0,1:T(8,128)(2,1)S(1)} %fusion.40), kind=kOutput, calls=%fused_computation.110 | convolution fusion | flops 1091567616 | bytes 4721152 | tf_op jit(solution)/shard_map/dot_general | solution.py:150
  1150.3 19.0 %fusion.38 = bf16[1,512,2048]{2,1,0:T(8,128)(2,1)} fusion(f32[512,2048]{1,0:T(8,128)S(1)} %fusion.52, f32[512,2048]{1,0:T(8,128)S(1)} %fusion.54, f32[512,2048]{1,0:T(8,128)S(1)} %fusion.53, s32[512]{0:T(512)S(1)} %add_select_fusion.4, pred[512]{0:T(512)(128)(4,1)S(1)} %fusion.63, bf16[512,2048]{0,1:T(8,128)(2,1)S(1)} %fusion.40), kind=kOutput, calls=%fused_computation.84 | convolution fusion | flops 1095761920 | bytes 15206912 | tf_op jit(solution)/shard_map/dot_general | solution.py:150
  (97 shorter events, 18.7 us)
Async XLA Ops:
  7.2 1.6 copy-start
  7.2 809.8 %all-gather.2.cloned.1.call-start = ((), (), s32[]{:S(2)}) async-start(), calls=%async_computation.2 | async-start | bytes 56623104 | tf_op jit(solution)/shard_map/all_gather | solution.py:124
  7.2 19.0 %copy-start.25 = (s32[512]{0:T(512)}, s32[512]{0:T(512)S(1)}, u32[]{:S(2)}) copy-start(s32[512]{0:T(512)S(1)} %add_select_fusion.7) | copy-start | bytes 6148
  7.3 19.0 %copy-start.27 = (pred[512]{0:T(512)(128)(4,1)}, pred[512]{0:T(512)(128)(4,1)S(1)}, u32[]{:S(2)}) copy-start(pred[512]{0:T(512)(128)(4,1)S(1)} %iota_compare_fusion) | copy-start | bytes 1540
  43.4 34.8 %copy-start.13 = (f32[512,512]{1,0:T(8,128)}, f32[512,512]{1,0:T(8,128)S(1)}, u32[]{:S(2)}) copy-start(f32[512,512]{1,0:T(8,128)S(1)} %fusion.48) | copy-start | bytes 3145732
  61.0 17.2 %copy-start.15 = (f32[512,512]{1,0:T(8,128)}, f32[512,512]{1,0:T(8,128)S(1)}, u32[]{:S(2)}) copy-start(f32[512,512]{1,0:T(8,128)S(1)} %fusion.46) | copy-start | bytes 3145732
  78.2 1.1 copy-start.17
  79.3 2.0 copy-start.3
  82.7 4.0 copy-start.5
  157.8 8.4 copy-start.24
  161.2 48.0 %collective-permute-start = (bf16[32,16,2048]{2,1,0:T(8,128)(2,1)S(1)}, bf16[32,16,2048]{2,1,0:T(8,128)(2,1)S(1)}, u32[]{:S(2)}, u32[]{:S(2)}) collective-permute-start(bf16[32,16,2048]{2,1,0:T(8,128)(2,1)S(1)} %bitcast.117), channel_id=1, source_target_pairs={{8,0},{16,8},{24,16},{32,24},{40,32},{48,40},{56,48},{64,56},{72,6... | collective-permute-start | bytes 6291464 | tf_op jit(solution)/shard_map/ppermute | solution.py:16
  163.6 49.6 %collective-permute-start.1 = (bf16[32,16,2048]{2,1,0:T(8,128)(2,1)S(1)}, bf16[32,16,2048]{2,1,0:T(8,128)(2,1)S(1)}, u32[]{:S(2)}, u32[]{:S(2)}) collective-permute-start(bf16[32,16,2048]{2,1,0:T(8,128)(2,1)S(1)} %bitcast.118), channel_id=1, source_target_pairs={{16,0},{24,8},{32,16},{40,24},{48,32},{56,40},{64,48},{72,56},{80,... | collective-permute-start | bytes 6291464 | tf_op jit(solution)/shard_map/ppermute | solution.py:16
  164.9 48.3 %collective-permute-start.2 = (bf16[32,16,2048]{2,1,0:T(8,128)(2,1)S(1)}, bf16[32,16,2048]{2,1,0:T(8,128)(2,1)S(1)}, u32[]{:S(2)}, u32[]{:S(2)}) collective-permute-start(bf16[32,16,2048]{2,1,0:T(8,128)(2,1)S(1)} %bitcast.119), channel_id=1, source_target_pairs={{24,0},{32,8},{40,16},{48,24},{56,32},{64,40},{72,48},{80,56},{88,... | collective-permute-start | bytes 6291464 | tf_op jit(solution)/shard_map/ppermute | solution.py:16
  256.7 1.9 copy-start.22
  256.7 2.2 copy-start.23
  256.7 2.5 copy-start.20
  256.7 2.8 copy-start.21
  846.3 1.6 copy-start.11
  846.3 2.2 copy-start.12
  919.9 76.3 %collective-permute-start.3 = (bf16[32,16,2048]{2,1,0:T(8,128)(2,1)S(1)}, bf16[32,16,2048]{2,1,0:T(8,128)(2,1)}, u32[]{:S(2)}, u32[]{:S(2)}) collective-permute-start(bf16[32,16,2048]{2,1,0:T(8,128)(2,1)S(1)} %pad_maximum_fusion.3), channel_id=1, source_target_pairs={{0,8},{8,16},{16,24},{24,32},{32,40},{40,48},{48,56},{56,64},{64,7... | collective-permute-start | bytes 6291464 | tf_op jit(solution)/shard_map/ppermute | solution.py:16
  923.7 8.7 copy-start.19
  923.7 87.3 %collective-permute-start.4 = (bf16[32,16,2048]{2,1,0:T(8,128)(2,1)S(1)}, bf16[32,16,2048]{2,1,0:T(8,128)(2,1)}, u32[]{:S(2)}, u32[]{:S(2)}) collective-permute-start(bf16[32,16,2048]{2,1,0:T(8,128)(2,1)S(1)} %pad_maximum_fusion.4), channel_id=1, source_target_pairs={{0,16},{8,24},{16,32},{24,40},{32,48},{40,56},{48,64},{56,72},{64,... | collective-permute-start | bytes 6291464 | tf_op jit(solution)/shard_map/ppermute | solution.py:16
  928.4 4.3 copy-start.9
  928.5 4.3 copy-start.10
  928.5 107.9 %collective-permute-start.5 = (bf16[32,16,2048]{2,1,0:T(8,128)(2,1)S(1)}, bf16[32,16,2048]{2,1,0:T(8,128)(2,1)}, u32[]{:S(2)}, u32[]{:S(2)}) collective-permute-start(bf16[32,16,2048]{2,1,0:T(8,128)(2,1)S(1)} %pad_maximum_fusion.5), channel_id=1, source_target_pairs={{0,24},{8,32},{16,40},{24,48},{32,56},{40,64},{48,72},{56,80},{64,... | collective-permute-start | bytes 6291464 | tf_op jit(solution)/shard_map/ppermute | solution.py:16
  932.7 20.6 %copy-start.7 = (f32[32,16,1024]{2,1,0:T(8,128)S(1)}, f32[32,16,1024]{2,1,0:T(8,128)}, u32[]{:S(2)}) copy-start(f32[32,16,1024]{2,1,0:T(8,128)} %get-tuple-element.68) | copy-start | bytes 6291460
  932.7 20.6 %copy-start.8 = (f32[32,16,1024]{2,1,0:T(8,128)S(1)}, f32[32,16,1024]{2,1,0:T(8,128)}, u32[]{:S(2)}) copy-start(f32[32,16,1024]{2,1,0:T(8,128)} %get-tuple-element.69) | copy-start | bytes 6291460
  953.4 20.6 %copy-start.18 = (bf16[16,16,2048]{2,1,0:T(8,128)(2,1)S(1)}, bf16[16,16,2048]{2,1,0:T(8,128)(2,1)}, u32[]{:S(2)}) copy-start(bf16[16,16,2048]{2,1,0:T(8,128)(2,1)} %get-tuple-element.42) | copy-start | bytes 3145732
  974.0 1.6 copy-start.4
  1042.1 36.6 %all-to-all-start.1 = ((bf16[32,16,2048]{2,1,0:T(8,128)(2,1)}), bf16[32,16,2048]{2,1,0:T(8,128)(2,1)S(1)}, u32[]{:S(2)}, u32[]{:S(2)}) async-start(bf16[32,16,2048]{2,1,0:T(8,128)(2,1)} %fusion.25), calls=%async_computation.1 | async-start | bytes 4194304 | tf_op jit(solution)/shard_map/all_to_all | solution.py:141
  1081.2 5.5 copy-start.14
  1081.2 5.5 copy-start.16
  1091.0 3.5 copy-start.2
  1091.0 4.1 copy-start.6
  1096.5 17.8 %copy-start.26 = (s32[512]{0:T(512)S(1)}, s32[512]{0:T(512)}, u32[]{:S(2)}) copy-start(s32[512]{0:T(512)} %copy-done.25) | copy-start | bytes 6148
  1096.5 17.8 %copy-start.28 = (pred[512]{0:T(512)(128)(4,1)S(1)}, pred[512]{0:T(512)(128)(4,1)}, u32[]{:S(2)}) copy-start(pred[512]{0:T(512)(128)(4,1)} %copy-done.27) | copy-start | bytes 1540
  1150.2 19.0 %copy-start.1 = (bf16[1,512,2048]{2,1,0:T(8,128)(2,1)S(1)}, bf16[1,512,2048]{2,1,0:T(8,128)(2,1)}, u32[]{:S(2)}) copy-start(bf16[1,512,2048]{2,1,0:T(8,128)(2,1)} %param.3) | copy-start | bytes 6291460
Sparse Core Ops, SparseCore 0:
  263.2 553.7 all-gather.1
